TPU v7x, 32 devices: a whole 2x2x4 slice. The times are simulated.
32 devices in a mesh: ta: 8 (over z, y), gx: 4 (over x, core).
Axes of the slice: x: 2, y: 2, z: 4, core: 2. Of those that a mesh axis runs over, the one named last changes fastest.
Arguments:
- right_side: float32 [64, 64, 64, 128], P('ta', 'gx'), may hold values from -6 to 6
- basis_x: float32 [64, 64], replicated, may hold values from -0.75 to 0.75
- basis_y: float32 [64, 64], replicated, may hold values from -0.75 to 0.75
- basis_z: float32 [128, 128], replicated, may hold values from -0.5 to 0.5
- eig_x: float32 [64], replicated, may hold values from 1 to 5.3312
- eig_y: float32 [64], replicated, may hold values from 1 to 5.3312
- eig_z: float32 [128], replicated, may hold values from 1 to 5.3312
- steps: float32 [64], replicated, may hold values from 0.25 to 1
Outputs:
- preconditioned: float32 [64, 64, 64, 128], P('ta', 'gx')
All inputs are finite; a program needn't handle non-finite values.
Results may differ from a plain program's by a relative error of at most 0.00012.
Values sent between devices are 32-bit elements; how exact they have to be, the bound alone decides.
A program may use at most 192 MiB of HBM per device.

v0:
```python
from functools import partial

import jax
import jax.numpy as jnp
from jax import lax
from jax.sharding import PartitionSpec as P

precise = lax.Precision.HIGHEST


def carried_in(value, axis, combine, identity, reverse):
    count, mine = (lax.axis_size(axis), lax.axis_index(axis))
    everything = jax.tree.map(lambda part: lax.all_gather(part, axis), value)
    start = jax.tree.map(
        lambda part, zero: jnp.broadcast_to(jnp.asarray(zero, part.dtype), part.shape),
        value,
        identity,
    )

    def step(k, before):
        at = count - 1 - k if reverse else k
        reached = at > mine if reverse else at < mine
        new = combine(before, jax.tree.map(lambda part: part[at], everything))
        return jax.tree.map(lambda a, b: jnp.where(reached, a, b), new, before)

    return lax.fori_loop(0, count, step, start)


def forward_yz(volume, basis_y, basis_z):
    halfway = jnp.einsum("tabc,cl->tabl", volume, basis_z, precision=precise)
    return jnp.einsum("tabc,bj->tajc", halfway, basis_y, precision=precise)


def backward_yz(volume, basis_y, basis_z):
    halfway = jnp.einsum("tajl,cl->tajc", volume, basis_z, precision=precise)
    return jnp.einsum("tajc,bj->tabc", halfway, basis_y, precision=precise)


def compose_affine(earlier, latter):
    return (latter[0] * earlier[0], latter[0] * earlier[1] + latter[1])


def compose_matrix(earlier, latter, degree):
    entries = []
    for row_at in range(degree):
        for col_at in range(degree):
            entries.append(
                sum(
                    (
                        latter[degree * row_at + inner_at] * earlier[degree * inner_at + col_at]
                        for inner_at in range(degree)
                    )
                )
            )
    factor = 1.0 / sum((jnp.abs(element) for element in entries))
    return tuple((element * factor for element in entries))


def local(right_side, basis_x, basis_y, basis_z, eig_x, eig_y, eig_z, steps):
    local_rows = right_side.shape[0]
    member = lax.axis_index("gx")
    chain_pos = lax.axis_index("ta")
    volume = forward_yz(right_side, basis_y, basis_z)
    spectral = jnp.einsum(
        "tabc,ai->tibc",
        lax.all_to_all(volume, "gx", split_axis=2, concat_axis=1, tiled=True),
        basis_x,
        precision=precise,
    )
    span_y = spectral.shape[2]
    part_y = lax.dynamic_slice_in_dim(eig_y, member * span_y, span_y)
    eigen_sum = eig_x[:, None, None] + part_y[None, :, None] + eig_z[None, None, :]
    total_rows = steps.shape[0]
    lengths = steps / total_rows
    padded = jnp.concatenate([lengths, jnp.zeros((1,), lengths.dtype)])
    first_row = chain_pos * local_rows
    current = lax.dynamic_slice_in_dim(padded, first_row, local_rows)
    following = lax.dynamic_slice_in_dim(padded, first_row + 1, local_rows)
    closing = jnp.where(
        first_row + jnp.arange(local_rows, dtype=jnp.int32) == total_rows - 1, 0.5, 0.0
    ).astype(lengths.dtype)
    all_ones = jnp.ones_like(eigen_sum)
    all_zeros = jnp.zeros_like(eigen_sum)

    def coefficients(cur_len, next_len, close_row):
        main_diag = eigen_sum * ((cur_len + next_len) / 3.0) + close_row
        sub_diag = eigen_sum * (cur_len / 6.0) - 0.5
        coupling = jnp.square(eigen_sum * (cur_len / 6.0)) - 0.25
        return (main_diag, sub_diag, coupling)

    def pivot_product(state_in, inputs):
        main_diag, sub_diag, coupling = coefficients(inputs[0], inputs[1], inputs[2])
        top_left, top_right, low_left, low_right = state_in
        new_left = main_diag * top_left - coupling * low_left
        new_right = main_diag * top_right - coupling * low_right
        factor = 1.0 / (
            jnp.abs(new_left) + jnp.abs(new_right) + jnp.abs(top_left) + jnp.abs(top_right)
        )
        return (
            (new_left * factor, new_right * factor, top_left * factor, top_right * factor),
            None,
        )

    identity = (all_ones, all_zeros, all_zeros, all_ones)
    local_map, unused = lax.scan(pivot_product, identity, (current, following, closing))
    before = carried_in(local_map, "ta", partial(compose_matrix, degree=2), identity, False)

    def eliminate(state_in, inputs):
        main_diag, sub_diag, coupling = coefficients(inputs[0], inputs[1], inputs[2])
        prev_top, prev_mid, slope_in, offset = state_in
        new_top = main_diag * prev_top - coupling * prev_mid
        pivot_now = new_top / prev_top
        new_slope = -sub_diag / pivot_now * slope_in
        new_offset = (inputs[3] - sub_diag * offset) / pivot_now
        factor = 1.0 / (jnp.abs(new_top) + jnp.abs(prev_top))
        return (
            (new_top * factor, prev_top * factor, new_slope, new_offset),
            (pivot_now, new_slope, new_offset),
        )

    final_state, (pivots, slopes, offsets) = lax.scan(
        eliminate,
        (before[0], before[2], all_ones, all_zeros),
        (current, following, closing, spectral),
    )
    carried = carried_in(
        (final_state[2], final_state[3]), "ta", compose_affine, (all_ones, all_zeros), False
    )
    eliminated = offsets + slopes * carried[1][None]

    def substitute(state_in, inputs):
        next_len, pivot_now, value_now = inputs
        super_diag = eigen_sum * (next_len / 6.0) + 0.5
        ratio_now = super_diag / pivot_now
        new_slope = -ratio_now * state_in[0]
        new_offset = value_now - ratio_now * state_in[1]
        return ((new_slope, new_offset), (new_slope, new_offset))

    first_map, (slopes_back, offsets_back) = lax.scan(
        substitute, (all_ones, all_zeros), (following, pivots, eliminated), reverse=True
    )
    later_carry = carried_in(first_map, "ta", compose_affine, (all_ones, all_zeros), True)
    solved = offsets_back + slopes_back * later_carry[1][None]
    cell_field = jnp.einsum("tibc,ai->tabc", solved, basis_x, precision=precise)
    return backward_yz(
        lax.all_to_all(cell_field, "gx", split_axis=1, concat_axis=2, tiled=True), basis_y, basis_z
    )


def solution(mesh):
    return jax.shard_map(
        local,
        mesh=mesh,
        in_specs=(P("ta", "gx", None, None), P(), P(), P(), P(), P(), P(), P()),
        out_specs=P("ta", "gx", None, None),
        check_vma=False,
    )
```

profile of v0, /device:TPU:1, one launch (start us, length us, event | category | flops | bytes accessed | tf_op | source)
XLA Modules:
  0.0 894.6 jit_solution(8667202025414751004)
XLA Ops:
  8.9 58.3 %while.115 = (s32[]{:T(128)}, f32[64,16,128]{2,1,0:T(8,128)S(1)}, f32[64,16,128]{2,1,0:T(8,128)S(1)}, f32[64,16,128]{2,1,0:T(8,128)S(1)}, f32[64,16,128]{2,1,0:T...) while((s32[]{:T(128)}, f32[64,16,128]{2,1,0:T(8,128)S(1)}, ...), condition=%wide.region_1.2_spmd.clone, body=%wide.region_0.1_spmd.clone.sunk | while | flops 5767174 | bytes 8398064 | solution.py:105
  70.1 6.5 fusion.48
  76.5 4.0 convolution_bitcast_fusion.2
  80.5 4.4 copy.28
  84.9 4.9 all-to-all-start
  90.1 47.3 %all-to-all-done = f32[8,16,64,128]{3,1,0,2:T(8,128)} async-done(((f32[8,16,64,128]{3,1,0,2:T(8,128)}), f32[8,16,64,128]{3,1,0,2:T(8,128)}, u32[]{:S(2)}, u32[]{:S(2)}) %all-to-all-start) | async-done | bytes 4194336 | tf_op jit(solution)/shard_map/all_to_all | solution.py:66
  140.3 5.3 convolution_bitcast_fusion.1
  145.6 69.6 %all-gather.19.cloned.1.call-done = f32[512,16,128]{2,1,0:T(8,128)} async-done(((f32[64,16,128]{2,1,0:T(8,128)}), f32[512,16,128]{2,1,0:T(8,128)}) %all-gather.19.cloned.1.call-update) | async-done | bytes 4194320 | tf_op jit(solution)/shard_map/all_gather | solution.py:13
  215.3 73.5 %all-gather.21.cloned.1.call-done = f32[512,16,128]{2,1,0:T(8,128)} async-done(((f32[64,16,128]{2,1,0:T(8,128)}), f32[512,16,128]{2,1,0:T(8,128)}) %all-gather.21.cloned.1.call-update) | async-done | bytes 4194320 | tf_op jit(solution)/shard_map/all_gather | solution.py:13
  288.7 73.3 %all-gather.23.cloned.1.call-done = f32[512,16,128]{2,1,0:T(8,128)} async-done(((f32[64,16,128]{2,1,0:T(8,128)}), f32[512,16,128]{2,1,0:T(8,128)}) %all-gather.23.cloned.1.call-update) | async-done | bytes 4194320 | tf_op jit(solution)/shard_map/all_gather | solution.py:13
  362.1 20.5 %while.116 = (s32[]{:T(128)}, f32[64,16,128]{2,1,0:T(8,128)S(1)}, f32[64,16,128]{2,1,0:T(8,128)S(1)}, f32[64,16,128]{2,1,0:T(8,128)S(1)}, f32[64,16,128]{2,1,0:T...) while((s32[]{:T(128)}, f32[64,16,128]{2,1,0:T(8,128)S(1)}, ...), condition=%wide.region_3.4_spmd.clone, body=%wide.region_2.3_spmd.clone.sunk | while | flops 4587524 | bytes 12058767 | solution.py:26
  389.7 65.6 %while.117 = (s32[]{:T(128)}, f32[64,16,128]{2,1,0:T(8,128)S(1)}, f32[64,16,128]{2,1,0:T(8,128)S(1)}, f32[64,16,128]{2,1,0:T(8,128)S(1)}, f32[64,16,128]{2,1,0:T...) while((s32[]{:T(128)}, f32[64,16,128]{2,1,0:T(8,128)S(1)}, ...), condition=%wide.region_5.6_spmd.clone, body=%wide.region_4.5_spmd.clone.sunk | while | flops 4718598 | bytes 8400135 | solution.py:121
  456.8 70.8 %all-gather.25.cloned.1.call-done = f32[512,16,128]{2,1,0:T(8,128)} async-done(((f32[64,16,128]{2,1,0:T(8,128)}), f32[512,16,128]{2,1,0:T(8,128)}) %all-gather.25.cloned.1.call-update) | async-done | bytes 4194320 | tf_op jit(solution)/shard_map/all_gather | solution.py:13
  527.6 73.3 %all-gather.27.cloned.1.call-done = f32[512,16,128]{2,1,0:T(8,128)} async-done(((f32[64,16,128]{2,1,0:T(8,128)}), f32[512,16,128]{2,1,0:T(8,128)}) %all-gather.27.cloned.1.call-update) | async-done | bytes 4194320 | tf_op jit(solution)/shard_map/all_gather | solution.py:13
  601.0 13.4 %while.118 = (s32[]{:T(128)}, f32[64,16,128]{2,1,0:T(8,128)S(1)}, s32[]{:T(128)}, f32[8,64,16,128]{3,2,1,0:T(8,128)}, f32[8,64,16,128]{3,2,1,0:T(8,128)}, /*index=5*/s32[]{:T(128)}, s32[]{:T(128)}) while((s32[]{:T(128)}, f32[64,16,128]{2,1,0:T(8,128)S(1)}, s32[]{:T(128)}, f32[8,64,16,128]{3,2,1,0:T(8,128)}, ...), condition=%wide.region_7.8_spmd.clone, body=%wide.region_6.7_spmd.clone.sunk | while | flops 524292 | bytes 2097253 | solution.py:26
  614.4 6.0 multiply_add_fusion.1
  625.1 30.7 %while.119 = (s32[]{:T(128)}, f32[64,16,128]{2,1,0:T(8,128)S(1)}, f32[64,16,128]{2,1,0:T(8,128)S(1)}, f32[8,64,16,128]{3,2,1,0:T(8,128)}, f32[8,64,16,128]{3,2,1...) while((s32[]{:T(128)}, f32[64,16,128]{2,1,0:T(8,128)S(1)}, ...), condition=%wide.region_9.10_spmd.clone, body=%wide.region_8.9_spmd.clone.sunk | while | flops 1310725 | bytes 4199607 | solution.py:139
  657.3 70.7 %all-gather.29.cloned.1.call-done = f32[512,16,128]{2,1,0:T(8,128)} async-done(((f32[64,16,128]{2,1,0:T(8,128)}), f32[512,16,128]{2,1,0:T(8,128)}) %all-gather.29.cloned.1.call-update) | async-done | bytes 4194320 | tf_op jit(solution)/shard_map/all_gather | solution.py:13
  728.1 73.5 %all-gather.31.cloned.1.call-done = f32[512,16,128]{2,1,0:T(8,128)} async-done(((f32[64,16,128]{2,1,0:T(8,128)}), f32[512,16,128]{2,1,0:T(8,128)}) %all-gather.31.cloned.1.call-update) | async-done | bytes 4194320 | tf_op jit(solution)/shard_map/all_gather | solution.py:13
  801.5 13.5 %while.120 = (s32[]{:T(128)}, f32[64,16,128]{2,1,0:T(8,128)S(1)}, s32[]{:T(128)}, f32[8,64,16,128]{3,2,1,0:T(8,128)}, f32[8,64,16,128]{3,2,1,0:T(8,128)}, /*index=5*/s32[]{:T(128)}, s32[]{:T(128)}, s32[]{:T(128)}, s32[]{:T(128)}) while((s32[]{:T(128)}, f32[64,16,128]{2,1,0:T(8,128)S(1)}, s32[]{:T(128)}, ...), condition=%wide.region_11.12_spmd.clone, body=%wide.region_10.11_spmd.clone.sunk | while | flops 524296 | bytes 2097315 | solution.py:26
  815.0 4.0 multiply_add_fusion
  819.1 5.1 fusion.43
  826.6 51.5 %all_to_all.36 = f32[8,64,16,128]{3,2,0,1:T(8,128)S(1)} all-to-all(f32[8,64,16,128]{3,2,0,1:T(8,128)S(1)} %copy.33), channel_id=1, replica_groups=mesh['ta'=8,'gx'=4] {'gx'}, dimensions={1} | all-to-all | bytes 8388608 | tf_op jit(solution)/shard_map/all_to_all | solution.py:146
  882.4 5.4 convolution_bitcast_fusion
  (213 shorter events, 194.6 us)
Async XLA Ops:
  6.5 63.5 %copy-start = (f32[128,128]{1,0:T(8,128)S(1)}, f32[128,128]{1,0:T(8,128)}, u32[]{:S(2)}) copy-start(f32[128,128]{1,0:T(8,128)} %param.23) | copy-start | bytes 196612
  6.5 139.1 %all-gather.17.cloned.1.call-start = ((), (), s32[]{:S(2)}) async-start(), calls=%async_computation.2 | async-start | bytes 4718592 | tf_op jit(solution)/shard_map/all_gather | solution.py:13
  67.2 0.8 copy-start.1
  67.2 1.0 copy-start.2
  67.2 1.6 copy-start.3
  67.2 2.3 copy-start.4
  68.0 147.3 %all-gather.19.cloned.1.call-start = ((), (), s32[]{:S(2)}) async-start(), calls=%async_computation.3 | async-start | bytes 4718592 | tf_op jit(solution)/shard_map/all_gather | solution.py:13
  68.7 220.0 %all-gather.21.cloned.1.call-start = ((), (), s32[]{:S(2)}) async-start(), calls=%async_computation.4 | async-start | bytes 4718592 | tf_op jit(solution)/shard_map/all_gather | solution.py:13
  69.5 292.6 %all-gather.23.cloned.1.call-start = ((), (), s32[]{:S(2)}) async-start(), calls=%async_computation.5 | async-start | bytes 4718592 | tf_op jit(solution)/shard_map/all_gather | solution.py:13
  70.1 6.5 copy-start.11
  84.9 52.5 %all-to-all-start = ((f32[8,16,64,128]{3,1,0,2:T(8,128)}), f32[8,16,64,128]{3,1,0,2:T(8,128)}, u32[]{:S(2)}, u32[]{:S(2)}) async-start(f32[8,16,64,128]{3,1,0,2:T(8,128)} %copy.28), calls=%async_computation | async-start | bytes 8388608 | tf_op jit(solution)/shard_map/all_to_all | solution.py:66
  89.8 437.8 %all-gather.25.cloned.1.call-start = ((), (), s32[]{:S(2)}) async-start(), calls=%async_computation.6 | async-start | bytes 4718592 | tf_op jit(solution)/shard_map/all_gather | solution.py:13
  137.4 2.8 copy-start.10
  385.1 4.7 copy-start.9
  455.3 0.8 copy-start.5
  455.4 1.0 copy-start.6
  456.2 144.8 %all-gather.27.cloned.1.call-start = ((), (), s32[]{:S(2)}) async-start(), calls=%async_computation.7 | async-start | bytes 4718592 | tf_op jit(solution)/shard_map/all_gather | solution.py:13
  456.7 271.3 %all-gather.29.cloned.1.call-start = ((), (), s32[]{:S(2)}) async-start(), calls=%async_computation.8 | async-start | bytes 4718592 | tf_op jit(solution)/shard_map/all_gather | solution.py:13
  655.7 0.8 copy-start.7
  655.7 1.1 copy-start.8
  656.6 145.0 %all-gather.31.cloned.1.call-start = ((), (), s32[]{:S(2)}) async-start(), calls=%async_computation.9 | async-start | bytes 4718592 | tf_op jit(solution)/shard_map/all_gather | solution.py:13
Sparse Core Ops, SparseCore 0:
  68.1 73.6 all-gather.16
  143.9 71.3 all-gather.18
  217.4 71.3 all-gather.20
  290.7 71.3 all-gather.22
  456.3 71.3 all-gather.24
  529.6 71.3 all-gather.26
  656.7 71.3 all-gather.28
  730.2 71.3 all-gather.30
where the time goes:
time: 898 us; the launch traced here: 895 us
  waiting for transfers between devices  555 us (62%)
  other arithmetic  133 us (15%)
  local copies, waits for them, and re-layouts  68.9 us (8%)
  blocking collectives  51.5 us (6%)
  loops' own time  36.9 us (4%)
  matrix products  29.9 us (3%)
  between operations  13.8 us (2%)
    all_gather x8, waiting for transfers between devices, carried_in(): everything = jax.tree.map(lambda part: lax.all_gather(part, axis), value)  505 us
    all_to_all x1, blocking collectives, local(): lax.all_to_all(cell_field, 'gx', split_axis=1, concat_axis=2, tiled=True)  51.5 us
    all_to_all x1, waiting for transfers between devices, local(): lax.all_to_all(volume, 'gx', split_axis=2, concat_axis=1, tiled=True)  47.3 us
    select_n x32, other arithmetic, step(): return jax.tree.map(lambda a, b: jnp.where(reached, a, b), new, before)  46.8 us
    dynamic_update_slice x16, other arithmetic, local(): lax.scan(eliminate, (before[0], before[2], all_ones, all_zeros), (current...  38.6 us
    dynamic_slice x56, local copies, waits for them, and re-layouts, local(): lax.scan(pivot_product, identity, (current, following, closing))  34.6 us
  transfers between devices with their start and end apart: 9, of which 8 were waited for; matrix products, arithmetic and copies ran while one was open for 3% of the time, Pallas kernels for 0%

commit v1 on v0

v1 whole, which is shorter than its diff:
```python
from functools import partial

import jax
import jax.numpy as jnp
from jax import lax
from jax.experimental import pallas as pl
from jax.experimental.pallas import tpu as pltpu
from jax.sharding import PartitionSpec as P

MESH = pl.DeviceIdType.MESH
SUB = 8
WAVE = 3
BF = jnp.bfloat16
F32 = jnp.float32


def halves(value):
    high = value.astype(BF)
    low = (value - high.astype(F32)).astype(BF)
    return high, low


def dot(a, b):
    return jnp.dot(a, b, preferred_element_type=F32)


def left(matrix, value):
    high, low = halves(value)
    return dot(matrix, jnp.concatenate([high, low, high], axis=0))


def right(value, twice, rest):
    high, low = halves(value)
    return dot(jnp.concatenate([high, low], axis=1), twice) + dot(high, rest)


def kernel(
    chain, cols, chunks, group,
    x_ref, zf1, zf2, zb1, zb2, yf, yb, xf, xb, exz, eig_y, mains, sixth, square, closing,
    out_ref,
    field, fsend, frecv, modal, rd, w, e, rdb, wb, last, sig, rho, gs, gr, hs, hr, bsend, brecv,
    in_sem, out_sem, fs_sem, fr_sem, fl_sem, bs_sem, br_sem, bl_sem, gs_sem, gr_sem, hs_sem, hr_sem,
):
    pos, me = lax.axis_index("ta"), lax.axis_index("gx")
    rows, block, ny, nz = field.shape
    nx = exz.shape[0]
    span = chunks * SUB
    up, down = lax.rem(pos + 1, chain), lax.rem(pos + chain - 1, chain)

    def load(t):
        return pltpu.make_async_copy(x_ref.at[t], field.at[t], in_sem.at[t])

    for t in range(rows):
        load(t).start()

    barrier = pltpu.get_barrier_semaphore()
    for d in range(1, cols):
        pl.semaphore_signal(barrier, inc=1, device_id={"gx": lax.rem(me + d, cols)}, device_id_type=MESH)
    for other in (up, down):
        pl.semaphore_signal(barrier, inc=1, device_id={"ta": other}, device_id_type=MESH)
    pl.semaphore_wait(barrier, cols + 1)

    def forward_copy(c, g, d, receive):
        times = pl.ds(g * group, group)
        to, here = lax.rem(me + d, cols), me
        if receive:
            to, here = me, lax.rem(me + cols - d, cols)
        return pltpu.make_async_remote_copy(
            src_ref=fsend.at[to, c, times], dst_ref=frecv.at[here, c, times],
            send_sem=fs_sem.at[c, g, d - 1], recv_sem=fr_sem.at[c, g, d - 1],
            device_id={"gx": lax.rem(me + d, cols)}, device_id_type=MESH,
        )

    def forward_own(c, g):
        times = pl.ds(g * group, group)
        return pltpu.make_async_copy(fsend.at[me, c, times], frecv.at[me, c, times], fl_sem.at[c, g])

    def start_forward(c, g):
        for d in range(1, cols):
            forward_copy(c, g, d, False).start()
        forward_own(c, g).start()

    def transform(g, carry):
        for k in range(group):
            t = g * group + k
            load(t).wait()
            for first in range(0, block, 4):
                value = field[t, first : first + 4].reshape(4 * ny, nz)
                value = right(value, zf1[...], zf2[...])
                for a in range(4):
                    y = left(yf[...], value[a * ny : (a + 1) * ny])
                    for q in range(cols):
                        for c in range(chunks):
                            at = (q * chunks + c) * SUB
                            fsend[q, c, t, pl.ds(first + a, SUB, stride=block), :] = y[at : at + SUB]
        start_forward(0, g)
        return carry

    lax.fori_loop(0, rows // group, transform, 0)
    for c in range(1, chunks):
        for g in range(rows // group):
            start_forward(c, g)

    def shift_of(c, j):
        return exz[...] + eig_y[me * span + c * SUB + j]

    def matrices(n, carry):
        c, j = n // SUB, lax.rem(n, SUB)
        s = shift_of(c, j)
        s2 = s * s
        own = pl.ds(pl.multiple_of(j * nx, nx), nx)

        def coupling(k):
            return s2 * square[k] - 0.25

        def before(q, ratio):
            one, two = jnp.ones_like(s), ratio
            for r in range(rows):
                k = q * rows + r
                one, two = (s * mains[k]) * one - coupling(k) * two, one
            return two / one

        def after(n, ratio):
            q = chain - 1 - n
            one, two = jnp.ones_like(s), ratio
            for r in range(rows - 1, -1, -1):
                k = q * rows + r
                one, two = (s * mains[k] + closing[k]) * one - coupling(k + 1) * two, one
            return two / one

        ratio = lax.fori_loop(0, pos, before, jnp.zeros_like(s))
        product = None
        for r in range(rows):
            k = pos * rows + r
            ratio = 1.0 / (s * mains[k] + closing[k] - coupling(k) * ratio)
            rd[c, r, own] = ratio
            weight = (0.5 - s * sixth[k]) * ratio
            w[c, r, own] = weight
            product = weight if product is None else product * weight
            carry_over = (s * sixth[k + 1] + 0.5) * ratio
            e[c, r, own] = carry_over
        sig[c, j] = product
        ratio = lax.fori_loop(0, chain - 1 - pos, after, jnp.zeros_like(s))
        end = pos * rows + rows
        last[c, j] = 1.0 / (1.0 - carry_over * ((s * sixth[end] - 0.5) * ratio))
        product = None
        for r in range(rows - 1, -1, -1):
            k = pos * rows + r
            ratio = 1.0 / (s * mains[k] + closing[k] - coupling(k + 1) * ratio)
            rdb[c, r, own] = ratio
            weight = -(s * sixth[k + 1] + 0.5) * ratio
            wb[c, r, own] = weight
            product = weight if product is None else product * weight
        rho[c, j] = product
        return carry

    lax.fori_loop(0, span, matrices, 0)

    def chain_copy(send, receive, s_sem, r_sem, c, j, other):
        return pltpu.make_async_remote_copy(
            src_ref=send.at[c, j], dst_ref=receive.at[c, j], send_sem=s_sem.at[c, j], recv_sem=r_sem.at[c, j],
            device_id={"ta": other}, device_id_type=MESH,
        )

    def upward(c, j):
        return chain_copy(gs, gr, gs_sem, gr_sem, c, j, up)

    def downward(c, j):
        return chain_copy(hs, hr, hs_sem, hr_sem, c, j, down)

    first, final = pos == 0, pos == chain - 1

    @pl.when(first)
    def _():
        gr[...] = jnp.zeros_like(gr)

    @pl.when(final)
    def _():
        hr[...] = jnp.zeros_like(hr)

    def back_copy(c, j, d, receive):
        to, here = lax.rem(me + d, cols), me
        if receive:
            to, here = me, lax.rem(me + cols - d, cols)
        part = pl.ds(pl.multiple_of(j * rows * block, rows * block), rows * block)
        return pltpu.make_async_remote_copy(
            src_ref=bsend.at[to, c, part], dst_ref=brecv.at[here, c, part],
            send_sem=bs_sem.at[c, j, d - 1], recv_sem=br_sem.at[c, j, d - 1],
            device_id={"gx": lax.rem(me + d, cols)}, device_id_type=MESH,
        )

    def back_own(c, j):
        part = pl.ds(pl.multiple_of(j * rows * block, rows * block), rows * block)
        return pltpu.make_async_copy(bsend.at[me, c, part], brecv.at[me, c, part], bl_sem.at[c, j])

    def chunk(c, carry):
        def arrive(g, carry):
            forward_own(c, g).wait()
            for d in range(1, cols):
                forward_copy(c, g, d, True).wait_recv()
            for k in range(group):
                t = g * group + k
                for j in range(SUB):
                    value = jnp.concatenate(
                        [frecv[q, c, t, j * block : (j + 1) * block, :] for q in range(cols)], axis=0
                    )
                    modal[t, j * nx : (j + 1) * nx] = left(xf[...], value)
            return carry

        lax.fori_loop(0, rows // group, arrive, 0)

        def maps(j, carry):
            own = pl.ds(pl.multiple_of(j * nx, nx), nx)
            g = modal[0, own] * rd[c, 0, own]
            for t in range(1, rows):
                g = modal[t, own] * rd[c, t, own] + w[c, t, own] * g
            gs[c, j] = g
            h = modal[rows - 1, own] * rdb[c, rows - 1, own]
            for t in range(rows - 2, -1, -1):
                h = modal[t, own] * rdb[c, t, own] + wb[c, t, own] * h
            hs[c, j] = h
            return carry

        lax.fori_loop(0, SUB, maps, 0)

        def tick(n, carry):
            j = n - WAVE * pos

            @pl.when((j >= 0) & (j < SUB))
            def _():
                @pl.when(pos > 0)
                def _():
                    upward(c, j).wait_recv()

                @pl.when(pos < chain - 1)
                def _():
                    gs[c, j] = gs[c, j] + sig[c, j] * gr[c, j]
                    upward(c, j).start()

            i = n - WAVE * (chain - 1 - pos)

            @pl.when((i >= 0) & (i < SUB))
            def _():
                @pl.when(pos < chain - 1)
                def _():
                    downward(c, i).wait_recv()

                @pl.when(pos > 0)
                def _():
                    hs[c, i] = hs[c, i] + rho[c, i] * hr[c, i]
                    downward(c, i).start()

            return carry

        lax.fori_loop(0, WAVE * (chain - 1) + SUB, tick, 0)

        def finish(j, carry):
            own = pl.ds(pl.multiple_of(j * nx, nx), nx)
            g = gr[c, j]
            for t in range(rows):
                g = modal[t, own] * rd[c, t, own] + w[c, t, own] * g
                modal[t, own] = g
            value = None
            for t in range(rows - 1, -1, -1):
                if value is None:
                    value = (g - e[c, t, own] * hr[c, j]) * last[c, j]
                else:
                    value = modal[t, own] - e[c, t, own] * value
                back = left(xb[...], value)
                at = pl.ds(pl.multiple_of((j * rows + t) * block, block), block)
                for q in range(cols):
                    bsend[q, c, at] = back[q * block : (q + 1) * block]
            for d in range(1, cols):
                back_copy(c, j, d, False).start()
            back_own(c, j).start()
            return carry

        lax.fori_loop(0, SUB, finish, 0)
        return carry

    lax.fori_loop(0, chunks, chunk, 0)

    def zstage(n, carry):
        c, j = n // SUB, lax.rem(n, SUB)
        back_own(c, j).wait()
        for d in range(1, cols):
            back_copy(c, j, d, True).wait_recv()
        part = pl.ds(pl.multiple_of(j * rows * block, rows * block), rows * block)
        for q in range(cols):
            brecv[q, c, part] = right(brecv[q, c, part], zb1[...], zb2[...])
        return carry

    lax.fori_loop(0, span, zstage, 0)

    def store(t):
        return pltpu.make_async_copy(field.at[t], out_ref.at[t], out_sem.at[t])

    def ystage(t, carry):
        for a in range(block):
            value = jnp.concatenate(
                [
                    brecv[q, c, pl.ds(t * block + a, SUB, stride=rows * block), :]
                    for q in range(cols)
                    for c in range(chunks)
                ],
                axis=0,
            )
            field[t, a] = left(yb[...], value)
        store(t).start()
        return carry

    lax.fori_loop(0, rows, ystage, 0)

    for c in range(chunks):
        for g in range(rows // group):
            for d in range(1, cols):
                forward_copy(c, g, d, False).wait_send()

    def drain(n, carry):
        c, j = n // SUB, lax.rem(n, SUB)
        for d in range(1, cols):
            back_copy(c, j, d, False).wait_send()

        @pl.when(pos < chain - 1)
        def _():
            upward(c, j).wait_send()

        @pl.when(pos > 0)
        def _():
            downward(c, j).wait_send()

        return carry

    lax.fori_loop(0, span, drain, 0)
    for t in range(rows):
        store(t).wait()


def parts(matrix):
    high = lax.reduce_precision(matrix, 8, 7)
    return high.astype(BF), (matrix - high).astype(BF)


def tripled(matrix):
    high, low = parts(matrix)
    return jnp.concatenate([high, high, low], axis=1)


def doubled(matrix):
    high, low = parts(matrix)
    return jnp.concatenate([high, high], axis=0), low


def local(chain, cols, right_side, basis_x, basis_y, basis_z, eig_x, eig_y, eig_z, steps):
    rows, block, ny, nz = right_side.shape
    nx = basis_x.shape[0]
    total = steps.shape[0]
    chunks = ny // cols // SUB
    group = 2 if rows % 2 == 0 else 1
    lengths = jnp.concatenate([steps / total, jnp.zeros((1,), steps.dtype)])
    mains = (lengths[:-1] + lengths[1:]) / 3.0
    sixth = lengths / 6.0
    closing = jnp.where(jnp.arange(total) == total - 1, 0.5, 0.0).astype(F32)
    vmem, smem, anywhere = (
        pl.BlockSpec(memory_space=pltpu.VMEM),
        pl.BlockSpec(memory_space=pltpu.SMEM),
        pl.BlockSpec(memory_space=pl.ANY),
    )
    modes = SUB * nx
    dma = pltpu.SemaphoreType.DMA
    table = pltpu.VMEM((chunks, rows, modes, nz), F32)
    tile = pltpu.VMEM((chunks, SUB, nx, nz), F32)
    travel = pltpu.VMEM((cols, chunks, rows, SUB * block, nz), F32)
    back = pltpu.VMEM((cols, chunks, SUB * rows * block, nz), F32)
    groups = rows // group
    return pl.pallas_call(
        partial(kernel, chain, cols, chunks, group),
        out_shape=jax.ShapeDtypeStruct(right_side.shape, F32),
        in_specs=[anywhere] + [vmem] * 9 + [smem] * 5,
        out_specs=anywhere,
        scratch_shapes=[
            pltpu.VMEM((rows, block, ny, nz), F32), travel, travel, pltpu.VMEM((rows, modes, nz), F32),
            table, table, table, table, table, tile, tile, tile, tile, tile, tile, tile, back, back,
            dma((rows,)), dma((rows,)),
            dma((chunks, groups, cols - 1)), dma((chunks, groups, cols - 1)), dma((chunks, groups)),
            dma((chunks, SUB, cols - 1)), dma((chunks, SUB, cols - 1)), dma((chunks, SUB)),
            dma((chunks, SUB)), dma((chunks, SUB)), dma((chunks, SUB)), dma((chunks, SUB)),
        ],
        compiler_params=pltpu.CompilerParams(
            collective_id=0, has_side_effects=True, vmem_limit_bytes=60 * 1024 * 1024
        ),
    )(
        right_side, *doubled(basis_z), *doubled(basis_z.T), tripled(basis_y.T), tripled(basis_y),
        tripled(basis_x.T), tripled(basis_x), eig_x[:, None] + eig_z[None, :],
        eig_y, mains, sixth, jnp.square(sixth), closing,
    )


def solution(mesh):
    return jax.shard_map(
        partial(local, mesh.shape["ta"], mesh.shape["gx"]),
        mesh=mesh,
        in_specs=(P("ta", "gx", None, None), P(), P(), P(), P(), P(), P(), P()),
        out_specs=P("ta", "gx", None, None),
        check_vma=False,
    )
```

time: 898 us -> 141 us (0.16)
  waiting for transfers between devices: 555 us -> 0 us
  Pallas kernels: 0 us -> 123 us
  other arithmetic: 133 us -> 10.2 us
  local copies, waits for them, and re-layouts: 68.9 us -> 7.38 us
  blocking collectives: 51.5 us -> 0 us
  loops' own time: 36.9 us -> 0 us
  matrix products: 29.9 us -> 0 us
  between operations: 13.8 us -> 0.04 us
    all_gather x8 -> x0, waiting for transfers between devices: 505 us -> none  [carried_in(): everything = jax.tree.map(lambda part: lax.all_gather(part, axis), value)]
    pallas_call x0 -> x1, Pallas kernels: none -> 123 us  [local(): pl.pallas_call(partial(kernel, chain, cols, chunks, group), out_shape=jax...]
    all_to_all x1 -> x0, blocking collectives: 51.5 us -> none  [local(): lax.all_to_all(cell_field, 'gx', split_axis=1, concat_axis=2, tiled=True)]
    all_to_all x1 -> x0, waiting for transfers between devices: 47.3 us -> none  [local(): lax.all_to_all(volume, 'gx', split_axis=2, concat_axis=1, tiled=True)]
    select_n x32 -> x1, other arithmetic: 46.8 us -> 1.26 us  [local(): closing = jnp.where(jnp.arange(total) == total - 1, 0.5, 0.0).astype(F32)]
    dynamic_slice x65 -> x0, local copies, waits for them, and re-layouts: 43.9 us -> none  [the longest x56 34.6 us: local(): lax.scan(pivot_product, identity, (current, following, closing))]
    dynamic_update_slice x16 -> x0, other arithmetic: 38.6 us -> none  [local(): lax.scan(eliminate, (before[0], before[2], all_ones, all_zeros), (current...]
    another operation x6 -> x0, loops' own time: 36.9 us -> none  [the longest x1 15.8 us: local(): lax.scan(eliminate, (before[0], before[2], all_ones, all_zeros), (current...]
  transfers between devices with their start and end apart: 9 -> 0, of which waited for: 8 -> 0; matrix products, arithmetic and copies ran while one was open for 3% -> 0% of each run, Pallas kernels for 0% -> 0%
where the time goes in v1:
time: 141 us; the launch traced here: 140 us
  Pallas kernels  123 us (87%)
  other arithmetic  10.2 us (7%)
  local copies, waits for them, and re-layouts  7.38 us (5%)
    pallas_call x1, Pallas kernels, local(): pl.pallas_call(partial(kernel, chain, cols, chunks, group), out_shape=jax...  123 us
    unnamed x4, local copies, waits for them, and re-layouts  7.38 us
    convert_element_type x5, other arithmetic, parts(): return (high.astype(BF), (matrix - high).astype(BF))  3.05 us

profile of v1, /device:TPU:1, one launch (start us, length us, event | category | flops | bytes accessed | tf_op | source)
XLA Modules:
  0.0 140.5 jit_solution(15112452730827443357)
XLA Ops:
  0.0 0.7 broadcast_multiply_fusion.1
  0.7 0.6 fusion.6
  1.3 0.6 broadcast_multiply_fusion.sixth
  1.9 1.3 compare_select_fusion
  3.1 1.4 broadcast_add_fusion.exz
  4.5 0.8 copy.11
  5.4 0.8 copy.10
  6.2 0.8 reduce-precision_convert_fusion.2
  7.0 0.7 pad_maximum_fusion.4
  7.7 0.8 reduce-precision_convert_fusion.4
  8.5 0.7 pad_maximum_fusion.2
  9.2 0.9 copy.9
  10.1 1.5 %fusion = (bf16[128,128]{1,0:T(8,128)(2,1)}, bf16[128,128]{1,0:T(8,128)(2,1)S(1)}, bf16[128,128]{1,0:T(8,128)(2,1)S(1)}, bf16[128,128]{1,0:T(8,128)(2,1)}) fusion(f32[128,128]{1,0:T(8,128)} %param.11, f32[128,128]{0,1:T(8,128)S(1)} %copy.9), kind=kLoop, calls=%fused_computation.4 | loop fusion | flops 131072 | bytes 262144 | tf_op jit(solution)/shard_map/convert_element_type | solution.py:341
  11.6 0.6 pad_maximum_fusion.zf1
  12.2 0.6 pad_maximum_fusion.1.zb1
  12.9 122.8 %shard_map.82 = f32[8,16,64,128]{3,2,1,0:T(8,128)} custom-call(f32[8,16,64,128]{3,2,1,0:T(8,128)} %x_ref.1, bf16[256,128]{1,0:T(8,128)(2,1)} %pad_maximum_fusion.zf1, bf16[128,128]{1,0:T(8,128)(2,1)} %get-tuple-element.9.zf2, bf16[256,128]{1,0:T(8,128)(2,1)} %pad_maximum_fusion.1.zb1, bf16[128,128]{1,0:T(8,128)(2,1)} %get-tuple-element.20.zb2, ...), custom_call_target="tpu_custom_call" | custom-call | tf_op jit(solution)/shard_map/pallas_call | solution.py:376
  135.7 4.8 %copy.13 = f32[8,16,64,128]{3,2,1,0:T(8,128)} copy(f32[8,16,64,128]{3,2,1,0:T(8,128)} %shard_map.82) | data formatting | bytes 8388608
  (2 shorter events, 0.0 us)

commit v2 on v1

--- a/solution.py
+++ b/solution.py
@@ -34,16 +34,27 @@
     return dot(jnp.concatenate([high, low], axis=1), twice) + dot(high, rest)
 
 
+def tripled(matrix):
+    high, low = halves(matrix)
+    return jnp.concatenate([high, high, low], axis=1)
+
+
+def doubled(matrix):
+    high, low = halves(matrix)
+    return jnp.concatenate([high, high], axis=0), low
+
+
 def kernel(
     chain, cols, chunks, group,
-    x_ref, zf1, zf2, zb1, zb2, yf, yb, xf, xb, exz, eig_y, mains, sixth, square, closing,
+    x_ref, basis_x, basis_y, basis_z, eig_x, eig_z, eig_y, steps,
     out_ref,
+    zf1, zf2, zb1, zb2, yf, yb, xf, xb, exz, mains, sixth, square,
     field, fsend, frecv, modal, rd, w, e, rdb, wb, last, sig, rho, gs, gr, hs, hr, bsend, brecv,
     in_sem, out_sem, fs_sem, fr_sem, fl_sem, bs_sem, br_sem, bl_sem, gs_sem, gr_sem, hs_sem, hr_sem,
 ):
     pos, me = lax.axis_index("ta"), lax.axis_index("gx")
     rows, block, ny, nz = field.shape
-    nx = exz.shape[0]
+    nx, total = exz.shape[0], chain * rows
     span = chunks * SUB
     up, down = lax.rem(pos + 1, chain), lax.rem(pos + chain - 1, chain)
 
@@ -59,6 +70,28 @@
     for other in (up, down):
         pl.semaphore_signal(barrier, inc=1, device_id={"ta": other}, device_id_type=MESH)
     pl.semaphore_wait(barrier, cols + 1)
+
+    zf1[...], zf2[...] = doubled(basis_z[...])
+    zb1[...], zb2[...] = doubled(basis_z[...].T)
+    yf[...], yb[...] = tripled(basis_y[...].T), tripled(basis_y[...])
+    xf[...], xb[...] = tripled(basis_x[...].T), tripled(basis_x[...])
+    diagonal = lax.broadcasted_iota(jnp.int32, (nx, nx), 0) == lax.broadcasted_iota(jnp.int32, (nx, nx), 1)
+    exz[...] = jnp.sum(jnp.where(diagonal, eig_x[...], 0.0), axis=1, keepdims=True) + eig_z[...]
+
+    def lengths(k, carry):
+        here = steps[k] * (1.0 / (6 * total))
+        after = jnp.where(k + 1 < total, steps[jnp.minimum(k + 1, total - 1)], 0.0) * (1.0 / (6 * total))
+        mains[k] = 2.0 * (here + after)
+        sixth[k] = here
+        square[k] = here * here
+        return carry
+
+    lax.fori_loop(0, total, lengths, 0)
+    sixth[total] = 0.0
+    square[total] = 0.0
+
+    def closing(k):
+        return jnp.where(k == total - 1, 0.5, 0.0)
 
     def forward_copy(c, g, d, receive):
         times = pl.ds(g * group, group)
@@ -125,14 +158,14 @@
             one, two = jnp.ones_like(s), ratio
             for r in range(rows - 1, -1, -1):
                 k = q * rows + r
-                one, two = (s * mains[k] + closing[k]) * one - coupling(k + 1) * two, one
+                one, two = (s * mains[k] + closing(k)) * one - coupling(k + 1) * two, one
             return two / one
 
         ratio = lax.fori_loop(0, pos, before, jnp.zeros_like(s))
         product = None
         for r in range(rows):
             k = pos * rows + r
-            ratio = 1.0 / (s * mains[k] + closing[k] - coupling(k) * ratio)
+            ratio = 1.0 / (s * mains[k] + closing(k) - coupling(k) * ratio)
             rd[c, r, own] = ratio
             weight = (0.5 - s * sixth[k]) * ratio
             w[c, r, own] = weight
@@ -146,7 +179,7 @@
         product = None
         for r in range(rows - 1, -1, -1):
             k = pos * rows + r
-            ratio = 1.0 / (s * mains[k] + closing[k] - coupling(k + 1) * ratio)
+            ratio = 1.0 / (s * mains[k] + closing(k) - coupling(k + 1) * ratio)
             rdb[c, r, own] = ratio
             weight = -(s * sixth[k + 1] + 0.5) * ratio
             wb[c, r, own] = weight
@@ -336,31 +369,12 @@
         store(t).wait()
 
 
-def parts(matrix):
-    high = lax.reduce_precision(matrix, 8, 7)
-    return high.astype(BF), (matrix - high).astype(BF)
-
-
-def tripled(matrix):
-    high, low = parts(matrix)
-    return jnp.concatenate([high, high, low], axis=1)
-
-
-def doubled(matrix):
-    high, low = parts(matrix)
-    return jnp.concatenate([high, high], axis=0), low
-
-
 def local(chain, cols, right_side, basis_x, basis_y, basis_z, eig_x, eig_y, eig_z, steps):
     rows, block, ny, nz = right_side.shape
     nx = basis_x.shape[0]
     total = steps.shape[0]
     chunks = ny // cols // SUB
     group = 2 if rows % 2 == 0 else 1
-    lengths = jnp.concatenate([steps / total, jnp.zeros((1,), steps.dtype)])
-    mains = (lengths[:-1] + lengths[1:]) / 3.0
-    sixth = lengths / 6.0
-    closing = jnp.where(jnp.arange(total) == total - 1, 0.5, 0.0).astype(F32)
     vmem, smem, anywhere = (
         pl.BlockSpec(memory_space=pltpu.VMEM),
         pl.BlockSpec(memory_space=pltpu.SMEM),
@@ -376,9 +390,13 @@
     return pl.pallas_call(
         partial(kernel, chain, cols, chunks, group),
         out_shape=jax.ShapeDtypeStruct(right_side.shape, F32),
-        in_specs=[anywhere] + [vmem] * 9 + [smem] * 5,
+        in_specs=[anywhere] + [vmem] * 5 + [smem] * 2,
         out_specs=anywhere,
         scratch_shapes=[
+            pltpu.VMEM((2 * nz, nz), BF), pltpu.VMEM((nz, nz), BF), pltpu.VMEM((2 * nz, nz), BF), pltpu.VMEM((nz, nz), BF),
+            pltpu.VMEM((ny, 3 * ny), BF), pltpu.VMEM((ny, 3 * ny), BF),
+            pltpu.VMEM((nx, 3 * nx), BF), pltpu.VMEM((nx, 3 * nx), BF), pltpu.VMEM((nx, nz), F32),
+            pltpu.SMEM((total,), F32), pltpu.SMEM((total + 1,), F32), pltpu.SMEM((total + 1,), F32),
             pltpu.VMEM((rows, block, ny, nz), F32), travel, travel, pltpu.VMEM((rows, modes, nz), F32),
             table, table, table, table, table, tile, tile, tile, tile, tile, tile, tile, back, back,
             dma((rows,)), dma((rows,)),
@@ -390,9 +408,7 @@
             collective_id=0, has_side_effects=True, vmem_limit_bytes=60 * 1024 * 1024
         ),
     )(
-        right_side, *doubled(basis_z), *doubled(basis_z.T), tripled(basis_y.T), tripled(basis_y),
-        tripled(basis_x.T), tripled(basis_x), eig_x[:, None] + eig_z[None, :],
-        eig_y, mains, sixth, jnp.square(sixth), closing,
+        right_side, basis_x, basis_y, basis_z, eig_x.reshape(1, nx), eig_z.reshape(1, nz), eig_y, steps
     )
 
 

time: 141 us -> 129 us (0.915)
  other arithmetic: 10.2 us -> 0 us
  local copies, waits for them, and re-layouts: 7.38 us -> 4.79 us
    convert_element_type x5 -> x0, other arithmetic: 3.05 us -> none  [parts(): return (high.astype(BF), (matrix - high).astype(BF))]
    concatenate x4 -> x0, other arithmetic: 2.69 us -> none  [the longest x2 1.44 us: tripled(): return jnp.concatenate([high, high, low], axis=1)]
    unnamed x4 -> x1, local copies, waits for them, and re-layouts: 7.38 us -> 4.79 us
where the time goes in v2:
time: 129 us; the launch traced here: 128 us
  Pallas kernels  124 us (96%)
  local copies, waits for them, and re-layouts  4.79 us (4%)
    pallas_call x1, Pallas kernels, local(): pl.pallas_call(partial(kernel, chain, cols, chunks, group), out_shape=jax...  124 us
    unnamed x1, local copies, waits for them, and re-layouts  4.79 us

profile of v2, /device:TPU:1, one launch (start us, length us, event | category | flops | bytes accessed | tf_op | source)
XLA Modules:
  0.0 128.4 jit_solution(13786128611598455586)
XLA Ops:
  0.0 123.6 %shard_map.82 = f32[8,16,64,128]{3,2,1,0:T(8,128)} custom-call(f32[8,16,64,128]{3,2,1,0:T(8,128)} %x_ref.1, f32[64,64]{1,0:T(8,128)} %basis_x.1, f32[64,64]{1,0:T(8,128)} %basis_y.1, f32[128,128]{1,0:T(8,128)} %basis_z.1, f32[1,64]{1,0:T(1,128)} %bitcast.2, f32[1,128]{1,0:T(1,128)} %bitcast.3, f32[64]{0:T(128)} %eig_y.1, f32[64]{0:T(128)} %steps.1), custom_call_target="tpu_custom_call" | custom-call | tf_op jit(solution)/shard_map/pallas_call | solution.py:390
  123.7 4.8 %copy.10 = f32[8,16,64,128]{3,2,1,0:T(8,128)} copy(f32[8,16,64,128]{3,2,1,0:T(8,128)} %shard_map.82) | data formatting | bytes 8388608

commit v3 on v2

--- a/solution.py
+++ b/solution.py
@@ -9,7 +9,7 @@
 
 MESH = pl.DeviceIdType.MESH
 SUB = 8
-WAVE = 3
+WAVE = 2
 BF = jnp.bfloat16
 F32 = jnp.float32
 
@@ -27,6 +27,12 @@
 def left(matrix, value):
     high, low = halves(value)
     return dot(matrix, jnp.concatenate([high, low, high], axis=0))
+
+
+def left_pair(matrix, one, two):
+    both = left(matrix, jnp.concatenate([one, two], axis=1))
+    width = one.shape[1]
+    return both[:, :width], both[:, width:]
 
 
 def right(value, twice, rest):
@@ -49,14 +55,18 @@
     x_ref, basis_x, basis_y, basis_z, eig_x, eig_z, eig_y, steps,
     out_ref,
     zf1, zf2, zb1, zb2, yf, yb, xf, xb, exz, mains, sixth, square,
-    field, fsend, frecv, modal, rd, w, e, rdb, wb, last, sig, rho, gs, gr, hs, hr, bsend, brecv,
+    field, fsend, frecv, modal, rd, w, e, rdb, wb, last, steps_own, steps_other, maps_own, maps_other, gs, gr, hs, hr, gin, hin,
+    bsend, brecv,
     in_sem, out_sem, fs_sem, fr_sem, fl_sem, bs_sem, br_sem, bl_sem, gs_sem, gr_sem, hs_sem, hr_sem,
+    ms_sem, mr_sem,
 ):
     pos, me = lax.axis_index("ta"), lax.axis_index("gx")
     rows, block, ny, nz = field.shape
     nx, total = exz.shape[0], chain * rows
     span = chunks * SUB
-    up, down = lax.rem(pos + 1, chain), lax.rem(pos + chain - 1, chain)
+    level, side, levels = pos // 2, lax.rem(pos, 2), chain // 2
+    partner = pos + 1 - 2 * side
+    up, down = lax.rem(pos + 2, chain), lax.rem(pos + chain - 2, chain)
 
     def load(t):
         return pltpu.make_async_copy(x_ref.at[t], field.at[t], in_sem.at[t])
@@ -67,9 +77,9 @@
     barrier = pltpu.get_barrier_semaphore()
     for d in range(1, cols):
         pl.semaphore_signal(barrier, inc=1, device_id={"gx": lax.rem(me + d, cols)}, device_id_type=MESH)
-    for other in (up, down):
+    for other in (partner, up, down):
         pl.semaphore_signal(barrier, inc=1, device_id={"ta": other}, device_id_type=MESH)
-    pl.semaphore_wait(barrier, cols + 1)
+    pl.semaphore_wait(barrier, cols + 2)
 
     zf1[...], zf2[...] = doubled(basis_z[...])
     zb1[...], zb2[...] = doubled(basis_z[...].T)
@@ -120,12 +130,15 @@
             for first in range(0, block, 4):
                 value = field[t, first : first + 4].reshape(4 * ny, nz)
                 value = right(value, zf1[...], zf2[...])
-                for a in range(4):
-                    y = left(yf[...], value[a * ny : (a + 1) * ny])
-                    for q in range(cols):
-                        for c in range(chunks):
-                            at = (q * chunks + c) * SUB
-                            fsend[q, c, t, pl.ds(first + a, SUB, stride=block), :] = y[at : at + SUB]
+                for a in range(0, 4, 2):
+                    pair = left_pair(
+                        yf[...], value[a * ny : (a + 1) * ny], value[(a + 1) * ny : (a + 2) * ny]
+                    )
+                    for k2, y in enumerate(pair):
+                        for q in range(cols):
+                            for c in range(chunks):
+                                at = (q * chunks + c) * SUB
+                                fsend[q, c, t, pl.ds(first + a + k2, SUB, stride=block), :] = y[at : at + SUB]
         start_forward(0, g)
         return carry
 
@@ -146,22 +159,26 @@
         def coupling(k):
             return s2 * square[k] - 0.25
 
-        def before(q, ratio):
-            one, two = jnp.ones_like(s), ratio
+        def before(q, state):
+            one, two = jnp.ones_like(s), state[0]
+            product = one
             for r in range(rows):
                 k = q * rows + r
-                one, two = (s * mains[k]) * one - coupling(k) * two, one
-            return two / one
-
-        def after(n, ratio):
-            q = chain - 1 - n
-            one, two = jnp.ones_like(s), ratio
+                one, two = (s * mains[k] + closing(k)) * one - coupling(k) * two, one
+                product = product * (0.5 - s * sixth[k])
+            return two / one, product / one
+
+        def after(q, state):
+            one, two = jnp.ones_like(s), state[0]
+            product = one
             for r in range(rows - 1, -1, -1):
                 k = q * rows + r
                 one, two = (s * mains[k] + closing(k)) * one - coupling(k + 1) * two, one
-            return two / one
-
-        ratio = lax.fori_loop(0, pos, before, jnp.zeros_like(s))
+                product = product * -(s * sixth[k + 1] + 0.5)
+            return two / one, product / one
+
+        start = (jnp.zeros_like(s), jnp.ones_like(s))
+        ratio, passed = lax.fori_loop(0, pos, before, start)
         product = None
         for r in range(rows):
             k = pos * rows + r
@@ -172,8 +189,13 @@
             product = weight if product is None else product * weight
             carry_over = (s * sixth[k + 1] + 0.5) * ratio
             e[c, r, own] = carry_over
-        sig[c, j] = product
-        ratio = lax.fori_loop(0, chain - 1 - pos, after, jnp.zeros_like(s))
+        steps_own[c, j, 0] = product
+        steps_other[c, j, 0] = lax.fori_loop(
+            0, 1 - side, lambda n, state: before(pos + 1, state), (ratio, passed)
+        )[1]
+        ratio, passed = lax.fori_loop(
+            0, chain - 1 - pos, lambda n, state: after(chain - 1 - n, state), start
+        )
         end = pos * rows + rows
         last[c, j] = 1.0 / (1.0 - carry_over * ((s * sixth[end] - 0.5) * ratio))
         product = None
@@ -184,10 +206,21 @@
             weight = -(s * sixth[k + 1] + 0.5) * ratio
             wb[c, r, own] = weight
             product = weight if product is None else product * weight
-        rho[c, j] = product
+        steps_own[c, j, 1] = product
+        steps_other[c, j, 1] = lax.fori_loop(
+            0, side, lambda n, state: after(pos - 1, state), (ratio, passed)
+        )[1]
         return carry
 
     lax.fori_loop(0, span, matrices, 0)
+
+    def maps_copy(c, j):
+        return pltpu.make_async_remote_copy(
+            src_ref=maps_own.at[c, j], dst_ref=maps_other.at[c, j],
+            send_sem=ms_sem.at[c, j], recv_sem=mr_sem.at[c, j],
+            device_id={"ta": partner}, device_id_type=MESH,
+        )
+
 
     def chain_copy(send, receive, s_sem, r_sem, c, j, other):
         return pltpu.make_async_remote_copy(
@@ -201,7 +234,7 @@
     def downward(c, j):
         return chain_copy(hs, hr, hs_sem, hr_sem, c, j, down)
 
-    first, final = pos == 0, pos == chain - 1
+    first, final = level == 0, level == levels - 1
 
     @pl.when(first)
     def _():
@@ -233,11 +266,13 @@
                 forward_copy(c, g, d, True).wait_recv()
             for k in range(group):
                 t = g * group + k
-                for j in range(SUB):
-                    value = jnp.concatenate(
-                        [frecv[q, c, t, j * block : (j + 1) * block, :] for q in range(cols)], axis=0
-                    )
-                    modal[t, j * nx : (j + 1) * nx] = left(xf[...], value)
+                for j in range(0, SUB, 2):
+                    pair = left_pair(xf[...], *(
+                        jnp.concatenate([frecv[q, c, t, i * block : (i + 1) * block, :] for q in range(cols)], axis=0)
+                        for i in (j, j + 1)
+                    ))
+                    for k2, value in enumerate(pair):
+                        modal[t, (j + k2) * nx : (j + k2 + 1) * nx] = value
             return carry
 
         lax.fori_loop(0, rows // group, arrive, 0)
@@ -247,68 +282,111 @@
             g = modal[0, own] * rd[c, 0, own]
             for t in range(1, rows):
                 g = modal[t, own] * rd[c, t, own] + w[c, t, own] * g
-            gs[c, j] = g
+            maps_own[c, j, 0] = g
             h = modal[rows - 1, own] * rdb[c, rows - 1, own]
             for t in range(rows - 2, -1, -1):
                 h = modal[t, own] * rdb[c, t, own] + wb[c, t, own] * h
-            hs[c, j] = h
+            maps_own[c, j, 1] = h
+            maps_copy(c, j).start()
             return carry
 
         lax.fori_loop(0, SUB, maps, 0)
 
-        def tick(n, carry):
-            j = n - WAVE * pos
-
-            @pl.when((j >= 0) & (j < SUB))
-            def _():
-                @pl.when(pos > 0)
-                def _():
-                    upward(c, j).wait_recv()
-
-                @pl.when(pos < chain - 1)
-                def _():
-                    gs[c, j] = gs[c, j] + sig[c, j] * gr[c, j]
-                    upward(c, j).start()
-
-            i = n - WAVE * (chain - 1 - pos)
-
-            @pl.when((i >= 0) & (i < SUB))
-            def _():
-                @pl.when(pos < chain - 1)
-                def _():
-                    downward(c, i).wait_recv()
-
-                @pl.when(pos > 0)
-                def _():
-                    hs[c, i] = hs[c, i] + rho[c, i] * hr[c, i]
-                    downward(c, i).start()
-
-            return carry
-
-        lax.fori_loop(0, WAVE * (chain - 1) + SUB, tick, 0)
-
-        def finish(j, carry):
+        def finish(j):
             own = pl.ds(pl.multiple_of(j * nx, nx), nx)
-            g = gr[c, j]
+            g = jnp.where(side == 0, gr[c, j], gin[c, j])
+            later = jnp.where(side == 1, hr[c, j], hin[c, j])
             for t in range(rows):
                 g = modal[t, own] * rd[c, t, own] + w[c, t, own] * g
                 modal[t, own] = g
-            value = None
+            value, waiting = None, []
             for t in range(rows - 1, -1, -1):
                 if value is None:
-                    value = (g - e[c, t, own] * hr[c, j]) * last[c, j]
+                    value = (g - e[c, t, own] * later) * last[c, j]
                 else:
                     value = modal[t, own] - e[c, t, own] * value
-                back = left(xb[...], value)
-                at = pl.ds(pl.multiple_of((j * rows + t) * block, block), block)
-                for q in range(cols):
-                    bsend[q, c, at] = back[q * block : (q + 1) * block]
+                waiting.append((t, value))
+                if len(waiting) == 2 or t == 0:
+                    if len(waiting) == 2:
+                        done = left_pair(xb[...], waiting[0][1], waiting[1][1])
+                    else:
+                        done = (left(xb[...], value),)
+                    for (t2, _), back in zip(waiting, done):
+                        at = pl.ds(pl.multiple_of((j * rows + t2) * block, block), block)
+                        for q in range(cols):
+                            bsend[q, c, at] = back[q * block : (q + 1) * block]
+                    waiting = []
             for d in range(1, cols):
                 back_copy(c, j, d, False).start()
             back_own(c, j).start()
+
+        def tick(n, carry):
+            @pl.when(n < SUB)
+            def _():
+                maps_copy(c, n).wait_recv()
+
+            j = n - WAVE * level
+
+            @pl.when((j >= 0) & (j < SUB))
+            def _():
+                @pl.when(level > 0)
+                def _():
+                    upward(c, j).wait_recv()
+
+                carried = gr[c, j]
+                kept, passed = maps_own[c, j, 0], maps_other[c, j, 0]
+                kept_step, passed_step = steps_own[c, j, 0], steps_other[c, j, 0]
+
+                @pl.when(side == 0)
+                def _():
+                    gs[c, j] = passed + passed_step * (kept + kept_step * carried)
+
+                @pl.when(side == 1)
+                def _():
+                    inner = passed + passed_step * carried
+                    gin[c, j] = inner
+                    gs[c, j] = kept + kept_step * inner
+
+                @pl.when(level < levels - 1)
+                def _():
+                    upward(c, j).start()
+
+            i = n - WAVE * (levels - 1 - level)
+
+            @pl.when((i >= 0) & (i < SUB))
+            def _():
+                @pl.when(level < levels - 1)
+                def _():
+                    downward(c, i).wait_recv()
+
+                carried = hr[c, i]
+                kept, passed = maps_own[c, i, 1], maps_other[c, i, 1]
+                kept_step, passed_step = steps_own[c, i, 1], steps_other[c, i, 1]
+
+                @pl.when(side == 1)
+                def _():
+                    hs[c, i] = passed + passed_step * (kept + kept_step * carried)
+
+                @pl.when(side == 0)
+                def _():
+                    inner = passed + passed_step * carried
+                    hin[c, i] = inner
+                    hs[c, i] = kept + kept_step * inner
+
+                @pl.when(level > 0)
+                def _():
+                    downward(c, i).start()
+
+            f = n - WAVE * jnp.maximum(level, levels - 1 - level)
+
+            @pl.when((f >= 0) & (f < SUB))
+            def _():
+                finish(f)
+
             return carry
 
-        lax.fori_loop(0, SUB, finish, 0)
+        lax.fori_loop(0, WAVE * (levels - 1) + SUB, tick, 0)
+
         return carry
 
     lax.fori_loop(0, chunks, chunk, 0)
@@ -329,16 +407,18 @@
         return pltpu.make_async_copy(field.at[t], out_ref.at[t], out_sem.at[t])
 
     def ystage(t, carry):
-        for a in range(block):
-            value = jnp.concatenate(
-                [
-                    brecv[q, c, pl.ds(t * block + a, SUB, stride=rows * block), :]
-                    for q in range(cols)
-                    for c in range(chunks)
-                ],
-                axis=0,
-            )
-            field[t, a] = left(yb[...], value)
+        for a in range(0, block, 2):
+            field[t, a], field[t, a + 1] = left_pair(yb[...], *(
+                jnp.concatenate(
+                    [
+                        brecv[q, c, pl.ds(t * block + i, SUB, stride=rows * block), :]
+                        for q in range(cols)
+                        for c in range(chunks)
+                    ],
+                    axis=0,
+                )
+                for i in (a, a + 1)
+            ))
         store(t).start()
         return carry
 
@@ -354,11 +434,13 @@
         for d in range(1, cols):
             back_copy(c, j, d, False).wait_send()
 
-        @pl.when(pos < chain - 1)
+        maps_copy(c, j).wait_send()
+
+        @pl.when(level < levels - 1)
         def _():
             upward(c, j).wait_send()
 
-        @pl.when(pos > 0)
+        @pl.when(level > 0)
         def _():
             downward(c, j).wait_send()
 
@@ -384,6 +466,7 @@
     dma = pltpu.SemaphoreType.DMA
     table = pltpu.VMEM((chunks, rows, modes, nz), F32)
     tile = pltpu.VMEM((chunks, SUB, nx, nz), F32)
+    twin = pltpu.VMEM((chunks, SUB, 2, nx, nz), F32)
     travel = pltpu.VMEM((cols, chunks, rows, SUB * block, nz), F32)
     back = pltpu.VMEM((cols, chunks, SUB * rows * block, nz), F32)
     groups = rows // group
@@ -398,11 +481,13 @@
             pltpu.VMEM((nx, 3 * nx), BF), pltpu.VMEM((nx, 3 * nx), BF), pltpu.VMEM((nx, nz), F32),
             pltpu.SMEM((total,), F32), pltpu.SMEM((total + 1,), F32), pltpu.SMEM((total + 1,), F32),
             pltpu.VMEM((rows, block, ny, nz), F32), travel, travel, pltpu.VMEM((rows, modes, nz), F32),
-            table, table, table, table, table, tile, tile, tile, tile, tile, tile, tile, back, back,
+            table, table, table, table, table, tile, twin, twin, twin, twin,
+            tile, tile, tile, tile, tile, tile, back, back,
             dma((rows,)), dma((rows,)),
             dma((chunks, groups, cols - 1)), dma((chunks, groups, cols - 1)), dma((chunks, groups)),
             dma((chunks, SUB, cols - 1)), dma((chunks, SUB, cols - 1)), dma((chunks, SUB)),
             dma((chunks, SUB)), dma((chunks, SUB)), dma((chunks, SUB)), dma((chunks, SUB)),
+            dma((chunks, SUB)), dma((chunks, SUB)),
         ],
         compiler_params=pltpu.CompilerParams(
             collective_id=0, has_side_effects=True, vmem_limit_bytes=60 * 1024 * 1024

time: 129 us -> 112 us (0.87)
  Pallas kernels: 124 us -> 107 us
    pallas_call x1, Pallas kernels: 124 us -> 107 us  [local(): pl.pallas_call(partial(kernel, chain, cols, chunks, group), out_shape=jax...]
where the time goes in v3:
time: 112 us
  Pallas kernels  107 us (96%)
  local copies, waits for them, and re-layouts  4.79 us (4%)
    pallas_call x1, Pallas kernels, local(): pl.pallas_call(partial(kernel, chain, cols, chunks, group), out_shape=jax...  107 us
    unnamed x1, local copies, waits for them, and re-layouts  4.79 us

profile of v3, /device:TPU:1, one launch (start us, length us, event | category | flops | bytes accessed | tf_op | source)
XLA Modules:
  0.0 112.2 jit_solution(17753740233042150401)
XLA Ops:
  0.0 107.4 %shard_map.82 = f32[8,16,64,128]{3,2,1,0:T(8,128)} custom-call(f32[8,16,64,128]{3,2,1,0:T(8,128)} %x_ref.1, f32[64,64]{1,0:T(8,128)} %basis_x.1, f32[64,64]{1,0:T(8,128)} %basis_y.1, f32[128,128]{1,0:T(8,128)} %basis_z.1, f32[1,64]{1,0:T(1,128)} %bitcast.2, f32[1,128]{1,0:T(1,128)} %bitcast.3, f32[64]{0:T(128)} %eig_y.1, f32[64]{0:T(128)} %steps.1), custom_call_target="tpu_custom_call" | custom-call | tf_op jit(solution)/shard_map/pallas_call | solution.py:473
  107.4 4.8 %copy.10 = f32[8,16,64,128]{3,2,1,0:T(8,128)} copy(f32[8,16,64,128]{3,2,1,0:T(8,128)} %shard_map.82) | data formatting | bytes 8388608

commit v4 on v3

--- a/solution.py
+++ b/solution.py
@@ -391,6 +391,10 @@
 
     lax.fori_loop(0, chunks, chunk, 0)
 
+    def store(c, j):
+        part = pl.ds(pl.multiple_of(j * rows * block, rows * block), rows * block)
+        return pltpu.make_async_copy(brecv.at[:, c, part], out_ref.at[:, c, part], out_sem.at[c, j])
+
     def zstage(n, carry):
         c, j = n // SUB, lax.rem(n, SUB)
         back_own(c, j).wait()
@@ -399,30 +403,10 @@
         part = pl.ds(pl.multiple_of(j * rows * block, rows * block), rows * block)
         for q in range(cols):
             brecv[q, c, part] = right(brecv[q, c, part], zb1[...], zb2[...])
+        store(c, j).start()
         return carry
 
     lax.fori_loop(0, span, zstage, 0)
-
-    def store(t):
-        return pltpu.make_async_copy(field.at[t], out_ref.at[t], out_sem.at[t])
-
-    def ystage(t, carry):
-        for a in range(0, block, 2):
-            field[t, a], field[t, a + 1] = left_pair(yb[...], *(
-                jnp.concatenate(
-                    [
-                        brecv[q, c, pl.ds(t * block + i, SUB, stride=rows * block), :]
-                        for q in range(cols)
-                        for c in range(chunks)
-                    ],
-                    axis=0,
-                )
-                for i in (a, a + 1)
-            ))
-        store(t).start()
-        return carry
-
-    lax.fori_loop(0, rows, ystage, 0)
 
     for c in range(chunks):
         for g in range(rows // group):
@@ -447,8 +431,18 @@
         return carry
 
     lax.fori_loop(0, span, drain, 0)
-    for t in range(rows):
-        store(t).wait()
+    for n in range(span):
+        store(n // SUB, n % SUB).wait()
+
+
+def last_stage(basis_y, field, out_ref):
+    basis = tripled(basis_y[...])
+    cols, chunks, _, _, block, nz = field.shape
+    for a in range(0, block, 2):
+        out_ref[0, a], out_ref[0, a + 1] = left_pair(basis, *(
+            jnp.concatenate([field[q, c, :, 0, i, :] for q in range(cols) for c in range(chunks)], axis=0)
+            for i in (a, a + 1)
+        ))
 
 
 def local(chain, cols, right_side, basis_x, basis_y, basis_z, eig_x, eig_y, eig_z, steps):
@@ -456,7 +450,7 @@
     nx = basis_x.shape[0]
     total = steps.shape[0]
     chunks = ny // cols // SUB
-    group = 2 if rows % 2 == 0 else 1
+    group = 1
     vmem, smem, anywhere = (
         pl.BlockSpec(memory_space=pltpu.VMEM),
         pl.BlockSpec(memory_space=pltpu.SMEM),
@@ -470,9 +464,9 @@
     travel = pltpu.VMEM((cols, chunks, rows, SUB * block, nz), F32)
     back = pltpu.VMEM((cols, chunks, SUB * rows * block, nz), F32)
     groups = rows // group
-    return pl.pallas_call(
+    field = pl.pallas_call(
         partial(kernel, chain, cols, chunks, group),
-        out_shape=jax.ShapeDtypeStruct(right_side.shape, F32),
+        out_shape=jax.ShapeDtypeStruct((cols, chunks, SUB * rows * block, nz), F32),
         in_specs=[anywhere] + [vmem] * 5 + [smem] * 2,
         out_specs=anywhere,
         scratch_shapes=[
@@ -483,7 +477,7 @@
             pltpu.VMEM((rows, block, ny, nz), F32), travel, travel, pltpu.VMEM((rows, modes, nz), F32),
             table, table, table, table, table, tile, twin, twin, twin, twin,
             tile, tile, tile, tile, tile, tile, back, back,
-            dma((rows,)), dma((rows,)),
+            dma((rows,)), dma((chunks, SUB)),
             dma((chunks, groups, cols - 1)), dma((chunks, groups, cols - 1)), dma((chunks, groups)),
             dma((chunks, SUB, cols - 1)), dma((chunks, SUB, cols - 1)), dma((chunks, SUB)),
             dma((chunks, SUB)), dma((chunks, SUB)), dma((chunks, SUB)), dma((chunks, SUB)),
@@ -495,6 +489,16 @@
     )(
         right_side, basis_x, basis_y, basis_z, eig_x.reshape(1, nx), eig_z.reshape(1, nz), eig_y, steps
     )
+    return pl.pallas_call(
+        last_stage,
+        grid=(rows,),
+        out_shape=jax.ShapeDtypeStruct(right_side.shape, F32),
+        in_specs=[
+            pl.BlockSpec((ny, ny), lambda t: (0, 0)),
+            pl.BlockSpec((cols, chunks, SUB, 1, block, nz), lambda t: (0, 0, 0, t, 0, 0)),
+        ],
+        out_specs=pl.BlockSpec((1, block, ny, nz), lambda t: (t, 0, 0, 0)),
+    )(basis_y, field.reshape(cols, chunks, SUB, rows, block, nz))
 
 
 def solution(mesh):

time: 112 us -> 112 us (level)
  local copies, waits for them, and re-layouts: 4.79 us -> 0 us
  Pallas kernels: 107 us -> 111 us
    pallas_call x0 -> x1, Pallas kernels: none -> 8.29 us  [local(): pl.pallas_call(last_stage, grid=(rows,), out_shape=jax.ShapeDtypeStruct(r...]
    unnamed x1 -> x0, local copies, waits for them, and re-layouts: 4.79 us -> none
    pallas_call x1, Pallas kernels: 107 us -> 103 us  [local(): pl.pallas_call(partial(kernel, chain, cols, chunks, group), out_shape=jax...]
where the time goes in v4:
time: 112 us; the launch traced here: 111 us
  Pallas kernels  111 us (99%)
    pallas_call x1, Pallas kernels, local(): pl.pallas_call(partial(kernel, chain, cols, chunks, group), out_shape=jax...  103 us
    pallas_call x1, Pallas kernels, local(): pl.pallas_call(last_stage, grid=(rows,), out_shape=jax.ShapeDtypeStruct(r...  8.29 us

profile of v4, /device:TPU:1, one launch (start us, length us, event | category | flops | bytes accessed | tf_op | source)
XLA Modules:
  0.0 111.4 jit_solution(16403709903485876348)
XLA Ops:
  0.0 103.1 %shard_map.82 = f32[4,2,1024,128]{3,2,1,0:T(8,128)} custom-call(f32[8,16,64,128]{3,2,1,0:T(8,128)} %x_ref.1, f32[64,64]{1,0:T(8,128)} %basis_x.1, f32[64,64]{1,0:T(8,128)} %basis_y.3, f32[128,128]{1,0:T(8,128)} %basis_z.1, f32[1,64]{1,0:T(1,128)} %bitcast.4, f32[1,128]{1,0:T(1,128)} %bitcast.5, f32[64]{0:T(128)} %eig_y.1, f32[64]{0:T(128)} %steps.1), custom_call_target="tpu_custom_call" | custom-call | tf_op jit(solution)/shard_map/pallas_call | solution.py:467
  103.1 8.3 %shard_map.83 = f32[8,16,64,128]{3,2,1,0:T(8,128)} custom-call(f32[64,64]{1,0:T(8,128)} %basis_y.3, f32[4,2,8,8,16,128]{5,4,3,2,1,0:T(8,128)} %bitcast.3), custom_call_target="tpu_custom_call" | custom-call | tf_op jit(solution)/shard_map/pallas_call | solution.py:492
